TPU v7x, 128 devices: a whole 4x4x4 slice. The times are simulated.
128 devices in a mesh: rows: 64 (over x, y_hi, z, core), grp: 2 (over y_lo).
Axes of the slice: x: 4, y: 4 (y_hi: 2, y_lo: 2; y = y_hi * 2 + y_lo), z: 4, core: 2. Of those that a mesh axis runs over, the one named last changes fastest.
Arguments:
- snapshots: float32 [524288, 256], P(('rows', 'grp'))
- blocks: bfloat16 [4096, 16, 128, 128], P(('rows', 'grp')), may hold values from -96 to 96
- columns: int32 [4096, 16], P(('rows', 'grp')), may hold values from 0 to 63
Outputs:
- projected: float32 [256, 256], replicated
- scaled_factor: float32 [256, 256], replicated
Inputs may be any that keep to these rules, and one draw needn't show every extreme that they name: `columns`: each stored block couples its block row to a block row of the same group of 2 * 32 consecutive block rows.
All inputs are finite; a program needn't handle non-finite values.
Results may differ from a plain program's by a relative error of at most 0.003.
Values may be sent and summed in bfloat16 or wider, within the bound.
No kernel may reach another device: no remote copies, remote signals or barrier semaphores. Data moves between devices by JAX's collectives and lax.ppermute only.
A program may use at most 192 MiB of HBM per device.

v0:
```python
import math
import jax
import jax.numpy as jnp
from jax import lax
from jax.sharding import PartitionSpec as P


def from_partner(value, axis, stride):
    mask = 2**stride
    pairs = [(source, source ^ mask) for source in range(lax.axis_size(axis))]
    return lax.ppermute(value, axis, pairs)


def inner_gram(left, right):
    return lax.dot_general(
        left,
        right,
        (((0,), (0,)), ((), ())),
        precision=lax.Precision.HIGHEST,
        preferred_element_type=jnp.float32,
    )


def upper_inverse(factor):
    size = factor.shape[0]
    unit_rows = jnp.eye(size, dtype=factor.dtype)

    def substitute(count, inverse):
        index = (size - 1 - count).astype(jnp.int32)
        frow = lax.dynamic_slice_in_dim(factor, index, 1, 0)
        unit = lax.dynamic_slice_in_dim(unit_rows, index, 1, 0)
        pivot = lax.dynamic_slice(factor, (index, index), (1, 1))
        fresh = (unit - jnp.dot(frow, inverse, precision=lax.Precision.HIGHEST)) / pivot
        return lax.dynamic_update_slice_in_dim(inverse, fresh, index, 0)

    return lax.fori_loop(jnp.int32(0), jnp.int32(size), substitute, jnp.zeros_like(factor))


def local(snapshots, blocks, columns):
    local_gram = inner_gram(snapshots, snapshots)
    factor = jnp.linalg.cholesky(local_gram).T
    levels = lax.axis_size(("rows", "grp")).bit_length() - 1
    for bit in range(levels):
        partner = from_partner(factor, ("rows", "grp"), bit)
        combined = inner_gram(factor, factor) + inner_gram(partner, partner)
        factor = jnp.linalg.cholesky(combined).T
    inverse = upper_inverse(factor)
    basis = jnp.dot(snapshots, inverse, precision=lax.Precision.HIGHEST)
    basis_half = basis.astype(jnp.bfloat16)
    block_len = blocks.shape[2]
    width = snapshots.shape[1]
    gathered = lax.all_gather(basis_half, "grp", axis=0, tiled=True)
    window = gathered.reshape(gathered.shape[0] // block_len, block_len, width)
    picked = jnp.take(window, columns, axis=0)
    image = jnp.einsum("bjrc,bjck->brk", blocks, picked, preferred_element_type=jnp.float32)
    image = image.reshape(snapshots.shape[0], width)
    partial_terms = inner_gram(basis, image)
    projected = lax.psum(partial_terms, ("rows", "grp"))
    total_rows = snapshots.shape[0] * lax.axis_size(("rows", "grp"))
    scaled_factor = factor / math.sqrt(total_rows)
    return (projected, scaled_factor)


def solution(mesh):
    return jax.shard_map(
        local,
        mesh=mesh,
        in_specs=(
            P(("rows", "grp"), None),
            P(("rows", "grp"), None, None, None),
            P(("rows", "grp"), None),
        ),
        out_specs=(P(), P()),
        check_vma=False,
    )
```

profile of v0, /device:TPU:1, one launch (start us, length us, event | category | flops | bytes accessed | tf_op | source)
XLA Modules:
  0.0 1051.1 jit_solution(15019776480115702252)
XLA Ops:
  7.2 10.4 fusion.133
  17.8 11.7 %cholesky.382 = f32[128,128]{1,0:T(8,128)S(1)} custom-call(f32[128,128]{1,0:T(8,128)S(1)} %cholesky.650), custom_call_target="Cholesky" | custom-call | tf_op jit(solution)/shard_map/jit(cholesky)/cholesky | solution.py:41
  29.5 9.8 custom-call.15
  39.8 11.7 %cholesky.399 = f32[128,128]{1,0:T(8,128)S(1)} custom-call(f32[128,128]{1,0:T(8,128)S(1)} %convolution_subtract_fusion.1), custom_call_target="Cholesky" | custom-call | tf_op jit(solution)/shard_map/jit(cholesky)/cholesky | solution.py:41
  54.7 2.4 collective-permute-start
  58.5 4.2 collective-permute-done
  63.3 11.7 %cholesky.416 = f32[128,128]{1,0:T(8,128)S(1)} custom-call(f32[128,128]{1,0:T(8,128)S(1)} %cholesky.653), custom_call_target="Cholesky" | custom-call | tf_op jit(solution)/shard_map/jit(cholesky)/cholesky | solution.py:46
  75.7 9.8 custom-call.16
  86.7 11.7 %cholesky.433 = f32[128,128]{1,0:T(8,128)S(1)} custom-call(f32[128,128]{1,0:T(8,128)S(1)} %slice_subtract_fusion.6), custom_call_target="Cholesky" | custom-call | tf_op jit(solution)/shard_map/jit(cholesky)/cholesky | solution.py:46
  102.7 1.9 collective-permute-start.1
  106.7 11.7 %cholesky.450 = f32[128,128]{1,0:T(8,128)S(1)} custom-call(f32[128,128]{1,0:T(8,128)S(1)} %cholesky.656), custom_call_target="Cholesky" | custom-call | tf_op jit(solution)/shard_map/jit(cholesky)/cholesky | solution.py:46
  119.2 9.8 custom-call.17
  130.1 11.7 %cholesky.467 = f32[128,128]{1,0:T(8,128)S(1)} custom-call(f32[128,128]{1,0:T(8,128)S(1)} %slice_subtract_fusion.5), custom_call_target="Cholesky" | custom-call | tf_op jit(solution)/shard_map/jit(cholesky)/cholesky | solution.py:46
  146.1 2.3 collective-permute-start.2
  149.9 5.2 collective-permute-done.2
  155.6 11.7 %cholesky.484 = f32[128,128]{1,0:T(8,128)S(1)} custom-call(f32[128,128]{1,0:T(8,128)S(1)} %cholesky.659), custom_call_target="Cholesky" | custom-call | tf_op jit(solution)/shard_map/jit(cholesky)/cholesky | solution.py:46
  168.1 9.8 custom-call.18
  179.0 11.7 %cholesky.501 = f32[128,128]{1,0:T(8,128)S(1)} custom-call(f32[128,128]{1,0:T(8,128)S(1)} %slice_subtract_fusion.4), custom_call_target="Cholesky" | custom-call | tf_op jit(solution)/shard_map/jit(cholesky)/cholesky | solution.py:46
  195.1 3.5 collective-permute-start.3
  200.0 4.4 collective-permute-done.3
  205.0 11.7 %cholesky.518 = f32[128,128]{1,0:T(8,128)S(1)} custom-call(f32[128,128]{1,0:T(8,128)S(1)} %cholesky.662), custom_call_target="Cholesky" | custom-call | tf_op jit(solution)/shard_map/jit(cholesky)/cholesky | solution.py:46
  217.5 9.8 custom-call.19
  228.4 11.7 %cholesky.535 = f32[128,128]{1,0:T(8,128)S(1)} custom-call(f32[128,128]{1,0:T(8,128)S(1)} %slice_subtract_fusion.3), custom_call_target="Cholesky" | custom-call | tf_op jit(solution)/shard_map/jit(cholesky)/cholesky | solution.py:46
  244.4 3.2 collective-permute-start.4
  249.1 3.5 collective-permute-done.4
  253.2 11.7 %cholesky.552 = f32[128,128]{1,0:T(8,128)S(1)} custom-call(f32[128,128]{1,0:T(8,128)S(1)} %cholesky.665), custom_call_target="Cholesky" | custom-call | tf_op jit(solution)/shard_map/jit(cholesky)/cholesky | solution.py:46
  265.7 9.8 custom-call.20
  276.6 11.7 %cholesky.569 = f32[128,128]{1,0:T(8,128)S(1)} custom-call(f32[128,128]{1,0:T(8,128)S(1)} %slice_subtract_fusion.2), custom_call_target="Cholesky" | custom-call | tf_op jit(solution)/shard_map/jit(cholesky)/cholesky | solution.py:46
  292.6 1.7 collective-permute-start.5
  295.7 2.6 collective-permute-done.5
  299.0 11.7 %cholesky.586 = f32[128,128]{1,0:T(8,128)S(1)} custom-call(f32[128,128]{1,0:T(8,128)S(1)} %cholesky.668), custom_call_target="Cholesky" | custom-call | tf_op jit(solution)/shard_map/jit(cholesky)/cholesky | solution.py:46
  311.4 9.8 custom-call.21
  322.4 11.7 %cholesky.603 = f32[128,128]{1,0:T(8,128)S(1)} custom-call(f32[128,128]{1,0:T(8,128)S(1)} %slice_subtract_fusion.1), custom_call_target="Cholesky" | custom-call | tf_op jit(solution)/shard_map/jit(cholesky)/cholesky | solution.py:46
  338.4 2.9 collective-permute-start.6
  342.8 2.6 collective-permute-done.6
  346.0 11.7 %cholesky.620 = f32[128,128]{1,0:T(8,128)S(1)} custom-call(f32[128,128]{1,0:T(8,128)S(1)} %cholesky.671), custom_call_target="Cholesky" | custom-call | tf_op jit(solution)/shard_map/jit(cholesky)/cholesky | solution.py:46
  357.8 9.8 custom-call.22
  368.0 11.7 %cholesky.637 = f32[128,128]{1,0:T(8,128)S(1)} custom-call(f32[128,128]{1,0:T(8,128)S(1)} %slice_subtract_fusion), custom_call_target="Cholesky" | custom-call | tf_op jit(solution)/shard_map/jit(cholesky)/cholesky | solution.py:46
  382.7 388.4 %while.12 = (s32[]{:T(128)}, f32[256,256]{1,0:T(8,128)S(1)}, f32[256,256]{1,0:T(8,128)S(1)}, f32[256,256]{1,0:T(8,128)S(1)}, s32[]{:T(128)}, /*index=5*/s32[]{:T(128)}, s32[]{:T(128)}, s32[]{:T(128)}) while((s32[]{:T(128)}, f32[256,256]{1,0:T(8,128)S(1)}, f32[256,256]{1,0:T(8,128)S(1)}, f32[256,256]{1,0:T(8,128)S(1)}, s32[]{:T(128)}, ...), condition=%wide.region_5.7_spmd, body=%wide.region_4.6_spmd.sunk | while | flops 786950 | bytes 268439 | solution.py:36
  771.1 8.6 fusion.134
  779.7 2.0 copy-done
  783.7 64.5 %all-gather.2.cloned.1.call-done = bf16[8192,256]{0,1:T(8,128)(2,1)} async-done(((bf16[4096,256]{0,1:T(8,128)(2,1)}), bf16[8192,256]{0,1:T(8,128)(2,1)}) %all-gather.2.cloned.1.call-update) | async-done | bytes 4194320 | tf_op jit(solution)/shard_map/all_gather | solution.py:52
  848.2 6.4 copy.73
  854.5 18.3 %gather_fusion = bf16[512,128,256]{2,1,0:T(8,128)(2,1)} fusion(bf16[64,128,256]{2,1,0:T(8,128)(2,1)} %bitcast.165, s32[1024]{0:T(1024)S(1)} %pad_clamp_fusion), kind=kCustom, calls=%fused_computation | custom fusion | bytes 67110912 | tf_op jit(solution)/shard_map/jit(_take)/gather | solution.py:54
  872.8 20.2 %fusion.4 = f32[32,256,128,1]{1,2,3,0:T(8,128)} fusion(bf16[32,16,128,128]{3,2,1,0:T(8,128)(2,1)} %param.7, bf16[32,16,128,256]{3,2,1,0:T(8,128)(2,1)} %bitcast.166, pred[32,16]{1,0:T(8,128)(4,1)S(1)} %copy.54), kind=kOutput, calls=%fused_computation.6 | convolution fusion | flops 4311744512 | bytes 54526464 | tf_op jit(solution)/shard_map/bjrc,bjck->brk/dot_general | solution.py:55
  893.1 6.6 fusion.135
  900.5 141.9 %all-reduce.3.cloned.1.call-done = f32[256,256]{1,0:T(8,128)} async-done(((f32[256,256]{1,0:T(8,128)}), f32[256,256]{1,0:T(8,128)}) %all-reduce.3.cloned.1.call-update) | async-done | bytes 262160 | tf_op jit(solution)/shard_map/psum | solution.py:58
  1042.4 1.7 copy.98
  (892 shorter events, 431.7 us)
Async XLA Ops:
  7.2 841.0 %all-gather.2.cloned.1.call-start = ((), (), s32[]{:S(2)}) async-start(), calls=%async_computation | async-start | bytes 6291456 | tf_op jit(solution)/shard_map/all_gather | solution.py:52
  51.6 2.1 copy-start.2
  54.7 8.0 collective-permute-start
  102.7 3.4 collective-permute-start.1
  146.1 8.9 collective-permute-start.2
  195.1 9.3 collective-permute-start.3
  244.4 8.2 collective-permute-start.4
  292.6 5.7 collective-permute-start.5
  338.4 7.0 collective-permute-start.6
  779.7 2.0 copy-start
  781.7 1.7 copy-start.3
  783.4 259.0 %all-reduce.3.cloned.1.call-start = ((), (), s32[]{:S(2)}) async-start(), calls=%async_computation.1 | async-start | bytes 524288 | tf_op jit(solution)/shard_map/psum | solution.py:58
  872.8 20.2 %copy-start.1 = (f32[256,4096]{1,0:T(8,128)S(1)}, f32[256,4096]{1,0:T(8,128)}, u32[]{:S(2)}) copy-start(f32[256,4096]{1,0:T(8,128)} %copy-done) | copy-start | bytes 12582916
Sparse Core Ops, SparseCore 0:
  783.5 64.6 all-gather.1
  899.8 142.5 all-reduce.2
where the time goes:
time: 1070 us; the launch traced here: 1050 us
  other arithmetic  289 us (27%)
  matrix products  279 us (26%)
  waiting for transfers between devices  229 us (21%)
  local copies, waits for them, and re-layouts  203 us (19%)
  between operations  25.5 us (2%)
  starting transfers between devices  17.9 us (2%)
    another operation x49, other arithmetic, local(): factor = jnp.linalg.cholesky(combined).T  246 us
    dot_general x256, matrix products, substitute(): jnp.dot(frow, inverse, precision=lax.Precision.HIGHEST)  213 us
    dynamic_slice x256, local copies, waits for them, and re-layouts, substitute(): pivot = lax.dynamic_slice(factor, (index, index), (1, 1))  152 us
    psum x1, waiting for transfers between devices, local(): projected = lax.psum(partial_terms, ('rows', 'grp'))  142 us
    all_gather x1, waiting for transfers between devices, local(): gathered = lax.all_gather(basis_half, 'grp', axis=0, tiled=True)  64.5 us
    another operation x6, other arithmetic, local(): factor = jnp.linalg.cholesky(local_gram).T  34 us
    dot_general x16, matrix products, inner_gram(): lax.dot_general(left, right, (((0,), (0,)), ((), ())), precision=lax.Prec...  29.9 us
    ppermute x7, waiting for transfers between devices, from_partner(): return lax.ppermute(value, axis, pairs)  22.4 us
  transfers between devices with their start and end apart: 9, of which 8 were waited for; matrix products, arithmetic and copies ran while one was open for 1% of the time, Pallas kernels for 0%

commit v1 on v0

--- a/solution.py
+++ b/solution.py
@@ -55,7 +55,8 @@
     image = jnp.einsum("bjrc,bjck->brk", blocks, picked, preferred_element_type=jnp.float32)
     image = image.reshape(snapshots.shape[0], width)
     partial_terms = inner_gram(basis, image)
-    projected = lax.psum(partial_terms, ("rows", "grp"))
+    partial = lax.psum(partial_terms, "rows")
+    projected = lax.psum(partial, "grp")
     total_rows = snapshots.shape[0] * lax.axis_size(("rows", "grp"))
     scaled_factor = factor / math.sqrt(total_rows)
     return (projected, scaled_factor)

time: 1070 us -> 1540 us (1.44)
  waiting for transfers between devices: 229 us -> 707 us
    psum x1 -> x2, waiting for transfers between devices: 142 us -> 620 us  [the longest x1 590 us: local(): partial = lax.psum(partial_terms, 'rows')]
  transfers between devices with their start and end apart: 9 -> 10, of which waited for: 8 -> 9; matrix products, arithmetic and copies ran while one was open for 1% -> 1% of each run, Pallas kernels for 0% -> 0%
where the time goes in v1:
time: 1540 us; the launch traced here: 1530 us
  waiting for transfers between devices  707 us (46%)
  other arithmetic  289 us (19%)
  matrix products  279 us (18%)
  local copies, waits for them, and re-layouts  203 us (13%)
  between operations  25.3 us (2%)
  starting transfers between devices  18 us (1%)
    psum x1, waiting for transfers between devices, local(): partial = lax.psum(partial_terms, 'rows')  590 us
    another operation x49, other arithmetic, local(): factor = jnp.linalg.cholesky(combined).T  246 us
    dot_general x256, matrix products, substitute(): jnp.dot(frow, inverse, precision=lax.Precision.HIGHEST)  213 us
    dynamic_slice x256, local copies, waits for them, and re-layouts, substitute(): pivot = lax.dynamic_slice(factor, (index, index), (1, 1))  152 us
    all_gather x1, waiting for transfers between devices, local(): gathered = lax.all_gather(basis_half, 'grp', axis=0, tiled=True)  64.5 us
    another operation x6, other arithmetic, local(): factor = jnp.linalg.cholesky(local_gram).T  34 us
  transfers between devices with their start and end apart: 10, of which 9 were waited for; matrix products, arithmetic and copies ran while one was open for 1% of the time, Pallas kernels for 0%

profile of v1, /device:TPU:1, one launch (start us, length us, event | category | flops | bytes accessed | tf_op | source)
XLA Modules:
  0.0 1529.3 jit_solution(8149049296241948254)
XLA Ops:
  7.2 10.4 fusion.133
  17.8 11.7 cholesky.382
  29.5 9.8 custom-call.15
  39.8 11.7 cholesky.399
  54.7 2.4 collective-permute-start
  58.5 4.2 collective-permute-done
  63.3 11.7 cholesky.416
  75.7 9.8 custom-call.16
  86.7 11.7 cholesky.433
  102.7 1.9 collective-permute-start.1
  106.7 11.7 cholesky.450
  119.2 9.8 custom-call.17
  130.1 11.7 cholesky.467
  146.1 2.3 collective-permute-start.2
  149.9 5.2 collective-permute-done.2
  155.6 11.7 cholesky.484
  168.1 9.8 custom-call.18
  179.0 11.7 cholesky.501
  195.1 3.5 collective-permute-start.3
  200.0 4.4 collective-permute-done.3
  205.0 11.7 cholesky.518
  217.5 9.8 custom-call.19
  228.4 11.7 cholesky.535
  244.4 3.2 collective-permute-start.4
  249.1 3.5 collective-permute-done.4
  253.2 11.7 cholesky.552
  265.7 9.8 custom-call.20
  276.6 11.7 cholesky.569
  295.7 2.6 collective-permute-done.5
  299.0 11.7 cholesky.586
  311.4 9.8 custom-call.21
  322.4 11.7 cholesky.603
  338.4 2.9 collective-permute-start.6
  342.8 2.6 collective-permute-done.6
  346.0 11.7 cholesky.620
  357.8 9.8 custom-call.22
  368.0 11.7 cholesky.637
  382.7 388.4 %while.12 = (s32[]{:T(128)}, f32[256,256]{1,0:T(8,128)S(1)}, f32[256,256]{1,0:T(8,128)S(1)}, f32[256,256]{1,0:T(8,128)S(1)}, s32[]{:T(128)}, /*index=5*/s32[]{:T(128)}, s32[]{:T(128)}, s32[]{:T(128)}) while((s32[]{:T(128)}, f32[256,256]{1,0:T(8,128)S(1)}, f32[256,256]{1,0:T(8,128)S(1)}, f32[256,256]{1,0:T(8,128)S(1)}, s32[]{:T(128)}, ...), condition=%wide.region_5.7_spmd, body=%wide.region_4.6_spmd.sunk | while | flops 786950 | bytes 268439 | solution.py:36
  771.1 8.6 fusion.134
  779.7 2.0 copy-done
  783.7 64.5 %all-gather.2.cloned.1.call-done = bf16[8192,256]{0,1:T(8,128)(2,1)} async-done(((bf16[4096,256]{0,1:T(8,128)(2,1)}), bf16[8192,256]{0,1:T(8,128)(2,1)}) %all-gather.2.cloned.1.call-update) | async-done | bytes 4194320 | tf_op jit(solution)/shard_map/all_gather | solution.py:52
  848.2 6.4 copy.73
  854.5 18.3 %gather_fusion = bf16[512,128,256]{2,1,0:T(8,128)(2,1)} fusion(bf16[64,128,256]{2,1,0:T(8,128)(2,1)} %bitcast.165, s32[1024]{0:T(1024)S(1)} %pad_clamp_fusion), kind=kCustom, calls=%fused_computation | custom fusion | bytes 67110912 | tf_op jit(solution)/shard_map/jit(_take)/gather | solution.py:54
  872.8 20.2 %fusion.4 = f32[32,256,128,1]{1,2,3,0:T(8,128)} fusion(bf16[32,16,128,128]{3,2,1,0:T(8,128)(2,1)} %param.7, bf16[32,16,128,256]{3,2,1,0:T(8,128)(2,1)} %bitcast.166, pred[32,16]{1,0:T(8,128)(4,1)S(1)} %copy.54), kind=kOutput, calls=%fused_computation.6 | convolution fusion | flops 4311744512 | bytes 54526464 | tf_op jit(solution)/shard_map/bjrc,bjck->brk/dot_general | solution.py:55
  893.1 6.6 fusion.135
  899.7 590.1 %all-reduce.4.cloned.1.call-done = f32[256,256]{1,0:T(8,128)} async-done(((f32[256,256]{1,0:T(8,128)}), f32[256,256]{1,0:T(8,128)}) %all-reduce.4.cloned.1.call-update) | async-done | bytes 262160 | tf_op jit(solution)/shard_map/psum | solution.py:58
  1490.7 30.2 %all-reduce.6.cloned.1.call-done = f32[256,256]{1,0:T(8,128)} async-done(((f32[256,256]{1,0:T(8,128)}), f32[256,256]{1,0:T(8,128)}) %all-reduce.6.cloned.1.call-update) | async-done | bytes 262160 | tf_op jit(solution)/shard_map/psum | solution.py:59
  1520.9 1.7 copy.99
  (895 shorter events, 433.4 us)
Async XLA Ops:
  7.2 841.0 %all-gather.2.cloned.1.call-start = ((), (), s32[]{:S(2)}) async-start(), calls=%async_computation | async-start | bytes 6291456 | tf_op jit(solution)/shard_map/all_gather | solution.py:52
  51.6 2.1 copy-start.2
  54.7 8.0 collective-permute-start
  102.7 3.4 collective-permute-start.1
  146.1 8.9 collective-permute-start.2
  195.1 9.3 collective-permute-start.3
  244.4 8.2 collective-permute-start.4
  292.6 5.7 collective-permute-start.5
  338.4 7.0 collective-permute-start.6
  779.7 2.0 copy-start
  781.7 1.7 copy-start.3
  783.4 706.4 %all-reduce.4.cloned.1.call-start = ((), (), s32[]{:S(2)}) async-start(), calls=%async_computation.1 | async-start | bytes 524288 | tf_op jit(solution)/shard_map/psum | solution.py:58
  872.8 20.2 %copy-start.1 = (f32[256,4096]{1,0:T(8,128)S(1)}, f32[256,4096]{1,0:T(8,128)}, u32[]{:S(2)}) copy-start(f32[256,4096]{1,0:T(8,128)} %copy-done) | copy-start | bytes 12582916
  899.7 621.3 %all-reduce.6.cloned.1.call-start = ((), (), s32[]{:S(2)}) async-start(), calls=%async_computation.2 | async-start | bytes 524288 | tf_op jit(solution)/shard_map/psum | solution.py:59
Sparse Core Ops, SparseCore 0:
  783.5 64.6 all-gather.1
  899.8 589.9 all-reduce.3
  1492.4 28.4 all-reduce.5

commit v2 on v0

--- a/solution.py
+++ b/solution.py
@@ -55,7 +55,7 @@
     image = jnp.einsum("bjrc,bjck->brk", blocks, picked, preferred_element_type=jnp.float32)
     image = image.reshape(snapshots.shape[0], width)
     partial_terms = inner_gram(basis, image)
-    projected = lax.psum(partial_terms, ("rows", "grp"))
+    projected = jnp.sum(lax.all_gather(partial_terms, axis_name=("rows", "grp")), axis=0)
     total_rows = snapshots.shape[0] * lax.axis_size(("rows", "grp"))
     scaled_factor = factor / math.sqrt(total_rows)
     return (projected, scaled_factor)

time: 1070 us -> 1280 us (1.20)
  waiting for transfers between devices: 229 us -> 436 us
  other arithmetic: 289 us -> 302 us
    all_gather x0 -> x1, waiting for transfers between devices: none -> 349 us  [local(): lax.all_gather(partial_terms, axis_name=('rows', 'grp'))]
    psum x1 -> x0, waiting for transfers between devices: 142 us -> none  [local(): projected = lax.psum(partial_terms, ('rows', 'grp'))]
where the time goes in v2:
time: 1280 us; the launch traced here: 1270 us
  waiting for transfers between devices  436 us (34%)
  other arithmetic  302 us (24%)
  matrix products  279 us (22%)
  local copies, waits for them, and re-layouts  202 us (16%)
  between operations  25.5 us (2%)
  starting transfers between devices  17.9 us (1%)
    all_gather x1, waiting for transfers between devices, local(): lax.all_gather(partial_terms, axis_name=('rows', 'grp'))  349 us
    another operation x49, other arithmetic, local(): factor = jnp.linalg.cholesky(combined).T  246 us
    dot_general x256, matrix products, substitute(): jnp.dot(frow, inverse, precision=lax.Precision.HIGHEST)  213 us
    dynamic_slice x256, local copies, waits for them, and re-layouts, substitute(): pivot = lax.dynamic_slice(factor, (index, index), (1, 1))  152 us
    all_gather x1, waiting for transfers between devices, local(): gathered = lax.all_gather(basis_half, 'grp', axis=0, tiled=True)  64.5 us
    another operation x6, other arithmetic, local(): factor = jnp.linalg.cholesky(local_gram).T  34 us
    dot_general x16, matrix products, inner_gram(): lax.dot_general(left, right, (((0,), (0,)), ((), ())), precision=lax.Prec...  29.9 us
  transfers between devices with their start and end apart: 9, of which 8 were waited for; matrix products, arithmetic and copies ran while one was open for 1% of the time, Pallas kernels for 0%

profile of v2, /device:TPU:1, one launch (start us, length us, event | category | flops | bytes accessed | tf_op | source)
XLA Modules:
  0.0 1269.4 jit_solution(11715629049904712082)
XLA Ops:
  7.2 10.4 fusion.133
  17.8 11.7 cholesky.382
  29.5 9.8 custom-call.15
  39.8 11.7 cholesky.399
  54.7 2.4 collective-permute-start
  58.5 4.2 collective-permute-done
  63.3 11.7 cholesky.416
  75.7 9.8 custom-call.16
  86.7 11.7 cholesky.433
  102.7 1.9 collective-permute-start.1
  106.7 11.7 cholesky.450
  119.2 9.8 custom-call.17
  130.1 11.7 cholesky.467
  146.1 2.3 collective-permute-start.2
  149.9 5.2 collective-permute-done.2
  155.6 11.7 cholesky.484
  168.1 9.8 custom-call.18
  179.0 11.7 cholesky.501
  195.1 3.5 collective-permute-start.3
  200.0 4.4 collective-permute-done.3
  205.0 11.7 cholesky.518
  217.5 9.8 custom-call.19
  228.4 11.7 cholesky.535
  244.4 3.2 collective-permute-start.4
  249.1 3.5 collective-permute-done.4
  253.2 11.7 cholesky.552
  265.7 9.8 custom-call.20
  276.6 11.7 cholesky.569
  292.6 1.7 collective-permute-start.5
  295.7 2.6 collective-permute-done.5
  299.0 11.7 cholesky.586
  311.4 9.8 custom-call.21
  322.4 11.7 cholesky.603
  338.4 2.9 collective-permute-start.6
  342.8 2.6 collective-permute-done.6
  346.0 11.7 cholesky.620
  357.8 9.8 custom-call.22
  368.0 11.7 cholesky.637
  382.7 388.4 %while.12 = (s32[]{:T(128)}, f32[256,256]{1,0:T(8,128)S(1)}, f32[256,256]{1,0:T(8,128)S(1)}, f32[256,256]{1,0:T(8,128)S(1)}, s32[]{:T(128)}, /*index=5*/s32[]{:T(128)}, s32[]{:T(128)}, s32[]{:T(128)}) while((s32[]{:T(128)}, f32[256,256]{1,0:T(8,128)S(1)}, f32[256,256]{1,0:T(8,128)S(1)}, f32[256,256]{1,0:T(8,128)S(1)}, s32[]{:T(128)}, ...), condition=%wide.region_5.7_spmd, body=%wide.region_4.6_spmd.sunk | while | flops 786950 | bytes 268439 | solution.py:36
  771.1 8.6 fusion.134
  779.7 2.0 copy-done
  783.7 64.5 %all-gather.4.cloned.1.call-done = bf16[8192,256]{0,1:T(8,128)(2,1)} async-done(((bf16[4096,256]{0,1:T(8,128)(2,1)}), bf16[8192,256]{0,1:T(8,128)(2,1)}) %all-gather.4.cloned.1.call-update) | async-done | bytes 4194320 | tf_op jit(solution)/shard_map/all_gather | solution.py:52
  848.2 6.4 copy.73
  854.5 18.3 %gather_fusion = bf16[512,128,256]{2,1,0:T(8,128)(2,1)} fusion(bf16[64,128,256]{2,1,0:T(8,128)(2,1)} %bitcast.166, s32[1024]{0:T(1024)S(1)} %pad_clamp_fusion), kind=kCustom, calls=%fused_computation | custom fusion | bytes 67110912 | tf_op jit(solution)/shard_map/jit(_take)/gather | solution.py:54
  872.8 20.2 %fusion.4 = f32[32,256,128,1]{1,2,3,0:T(8,128)} fusion(bf16[32,16,128,128]{3,2,1,0:T(8,128)(2,1)} %param.7, bf16[32,16,128,256]{3,2,1,0:T(8,128)(2,1)} %bitcast.167, pred[32,16]{1,0:T(8,128)(4,1)S(1)} %copy.54), kind=kOutput, calls=%fused_computation.6 | convolution fusion | flops 4311744512 | bytes 54526464 | tf_op jit(solution)/shard_map/bjrc,bjck->brk/dot_general | solution.py:55
  893.1 6.6 fusion.135
  900.5 349.2 %all-gather.6.cloned.1.call-done = f32[32768,256]{1,0:T(8,128)} async-done(((f32[256,256]{1,0:T(8,128)}), f32[32768,256]{1,0:T(8,128)}) %all-gather.6.cloned.1.call-update) | async-done | bytes 33554448 | tf_op jit(solution)/shard_map/all_gather | solution.py:58
  1249.7 12.7 reduce_sum.9
  (892 shorter events, 431.7 us)
Async XLA Ops:
  7.2 841.0 %all-gather.4.cloned.1.call-start = ((), (), s32[]{:S(2)}) async-start(), calls=%async_computation | async-start | bytes 6291456 | tf_op jit(solution)/shard_map/all_gather | solution.py:52
  51.6 2.1 copy-start.2
  54.7 8.0 collective-permute-start
  102.7 3.4 collective-permute-start.1
  146.1 8.9 collective-permute-start.2
  195.1 9.3 collective-permute-start.3
  244.4 8.2 collective-permute-start.4
  292.6 5.7 collective-permute-start.5
  338.4 7.0 collective-permute-start.6
  779.7 2.0 copy-start
  781.7 1.7 copy-start.3
  783.4 466.3 %all-gather.6.cloned.1.call-start = ((), (), s32[]{:S(2)}) async-start(), calls=%async_computation.1 | async-start | bytes 33816576 | tf_op jit(solution)/shard_map/all_gather | solution.py:58
  872.8 20.2 %copy-start.1 = (f32[256,4096]{1,0:T(8,128)S(1)}, f32[256,4096]{1,0:T(8,128)}, u32[]{:S(2)}) copy-start(f32[256,4096]{1,0:T(8,128)} %copy-done) | copy-start | bytes 12582916
Sparse Core Ops, SparseCore 0:
  783.5 64.6 all-gather.3
  899.8 349.8 all-gather.5
